TPU v7x, 512 devices: a whole 4x4x16 slice. The times are simulated.
512 devices in a mesh: quad: 16 (over z_lo, core), gy: 8 (over y, z_hi), gx: 4 (over x).
Axes of the slice: x: 4, y: 4, z: 16 (z_hi: 2, z_lo: 8; z = z_hi * 8 + z_lo), core: 2. Of those that a mesh axis runs over, the one named last changes fastest.
Arguments:
- modes_now: bfloat16 [1024, 64, 512], P('quad', 'gy', 'gx'), may hold values from -4 to 4
- basis_rows: bfloat16 [4096, 1024], P('quad'), may hold values from -0.25 to 0.25
- quad_weights: float32 [4096], P('quad'), may hold values from 0.2 to 2
- germ_nodes: float32 [4096, 8], P('quad'), may hold values from -1.5 to 1.5
- log_fields: float32 [8, 64, 512], P(None, 'gy', 'gx'), may hold values from -1 to 1
- reaction_rates: float32 [4096], P('quad'), may hold values from 0.08 to 0.32
Outputs:
- modes_next: float32 [1024, 64, 512], P('quad', 'gy', 'gx')
All inputs are finite; a program needn't handle non-finite values.
Results may differ from a plain program's by a relative error of at most 0.02.
Values may be sent and summed in bfloat16 or wider, within the bound.
No kernel may reach another device: no remote copies, remote signals or barrier semaphores. Data moves between devices by JAX's collectives and lax.ppermute only.
A program may use at most 64 MiB of HBM per device.

v0:
```python
import jax
import jax.numpy as jnp
from jax import lax
from jax.sharding import PartitionSpec as P

time_step = 0.04


def with_halo(array, sides, width):
    for axis, dim in sides:
        peers, length = (lax.axis_size(axis), array.shape[dim])
        up = [(i, (i + 1) % peers) for i in range(peers - 1)]
        down = [(j, i) for i, j in up]
        last = lax.slice_in_dim(array, length - width, length, axis=dim)
        leading = lax.slice_in_dim(array, 0, width, axis=dim)
        before = lax.ppermute(last, axis, up)
        after = lax.ppermute(leading, axis, down)
        array = jnp.concatenate([before, array, after], axis=dim)
    return array


def neighbour(array, drow, dcol):
    return array[:, 1 + drow : array.shape[1] - 1 + drow, 1 + dcol : array.shape[2] - 1 + dcol]


def drive_with(field_ext, coeff_ext, rates, weights):
    center = neighbour(field_ext, 0, 0)
    coeff_mid = neighbour(coeff_ext, 0, 0)
    total = jnp.zeros_like(center)
    for drow, dcol in ((-1, 0), (1, 0), (0, -1), (0, 1)):
        total = total + (coeff_mid + neighbour(coeff_ext, drow, dcol)) * (
            neighbour(field_ext, drow, dcol) - center
        )
    total = total + rates[:, None, None] * (center - center * center * center)
    return (weights[:, None, None] * total).astype(jnp.bfloat16).reshape(center.shape[0], -1)


def rim_fields(field):
    return with_halo(field, (("gy", 1), ("gx", 2)), 1)


def body(modes_now, basis_rows, quad_weights, germ_nodes, log_fields, reaction_rates):
    k_local, rows_y, cols_x = modes_now.shape
    q_local, modes_total = basis_rows.shape
    log_ext = with_halo(log_fields, (("gy", 1), ("gx", 2)), 1)
    coeff_ext = jnp.exp(
        jnp.einsum("qj,jyx->qyx", germ_nodes, log_ext, precision=lax.Precision.HIGHEST)
    )

    def realize(block_flat):
        return jnp.dot(
            basis_rows,
            lax.all_gather(block_flat, "quad", axis=0, tiled=True),
            preferred_element_type=jnp.float32,
        )

    def field_of(block):
        return rim_fields(realize(block.reshape(k_local, -1)).reshape(q_local, rows_y, cols_x))

    def drive(field_ext):
        return drive_with(field_ext, coeff_ext, reaction_rates, quad_weights)

    def spread(weighted):
        return (
            lax.psum_scatter(
                lax.dot_general(
                    basis_rows,
                    weighted,
                    (((0,), (0,)), ((), ())),
                    preferred_element_type=jnp.float32,
                ).astype(jnp.bfloat16),
                "quad",
                scatter_dimension=0,
                tiled=True,
            )
            .astype(jnp.float32)
            .reshape(k_local, rows_y, cols_x)
        )

    current = modes_now.astype(jnp.float32)
    first = spread(drive(field_of(modes_now)))
    iterate_one = (current + time_step * first).astype(jnp.bfloat16)
    field_one = field_of(iterate_one)
    second = spread(drive(field_one))
    return current + time_step * second


def solution(mesh):
    in_specs = (
        P("quad", "gy", "gx"),
        P("quad", None),
        P("quad"),
        P("quad", None),
        P(None, "gy", "gx"),
        P("quad"),
    )
    out_specs = P("quad", "gy", "gx")
    return jax.shard_map(body, mesh=mesh, in_specs=in_specs, out_specs=out_specs, check_vma=False)
```

profile of v0, /device:TPU:4, one launch (start us, length us, event | category | flops | bytes accessed | tf_op | source)
XLA Modules:
  0.0 528.8 jit_solution(11073676379611655207)
XLA Ops:
  6.5 0.0 copy-start
  6.5 0.0 all-gather.3.cloned.1.call-start
  6.5 1.6 copy.32
  8.2 0.0 all-gather.3.cloned.1.call-update
  8.2 0.0 reduce-scatter.7.cloned.1.call-start
  8.3 0.8 fusion.42
  9.1 15.7 %collective-permute-start = (f32[8,1,128]{2,0,1:T(8,128)S(1)}, f32[8,1,128]{2,0,1:T(8,128)S(1)}, u32[]{:S(2)}, u32[]{:S(2)}) collective-permute-start(f32[8,1,128]{2,0,1:T(8,128)S(1)} %copy.29), channel_id=1, source_target_pairs={{0,4},{4,8},{8,12},{12,16},{16,20},{20,24},{24,28},{1,5},{5,9},{9,... | collective-permute-start | bytes 12296 | tf_op jit(solution)/shard_map/ppermute | solution.py:16
  24.8 1.3 collective-permute-start.1
  26.1 0.0 collective-permute-done
  26.2 0.8 constant_dynamic-update-slice_fusion.1
  26.9 12.2 %collective-permute-done.1 = f32[8,1,128]{2,0,1:T(8,128)S(1)} collective-permute-done((f32[8,1,128]{2,0,1:T(8,128)S(1)}, f32[8,1,128]{2,0,1:T(8,128)S(1)}, u32[]{:S(2)}, u32[]{:S(2)}) %collective-permute-start.1) | collective-permute-done | bytes 4128 | tf_op jit(solution)/shard_map/ppermute | solution.py:17
  39.2 0.0 copy-start.2
  39.2 75.3 %all-gather.3.cloned.1.call-done = bf16[1024,1024]{1,0:T(8,128)(2,1)} async-done(((bf16[64,1024]{1,0:T(8,128)(2,1)}), bf16[1024,1024]{1,0:T(8,128)(2,1)}) %all-gather.3.cloned.1.call-update) | async-done | bytes 2097168 | tf_op jit(solution)/shard_map/all_gather | solution.py:53
  114.5 0.0 copy-done
  114.5 2.5 fusion.43
  117.0 0.0 copy-start.3
  117.0 0.0 copy-start.4
  117.1 16.9 %collective-permute-start.4 = (f32[256,1,128]{0,2,1:T(8,128)S(1)}, f32[256,1,128]{0,2,1:T(8,128)S(1)}, u32[]{:S(2)}, u32[]{:S(2)}) collective-permute-start(f32[256,1,128]{0,2,1:T(8,128)S(1)} %get-tuple-element.11), channel_id=1, source_target_pairs={{0,4},{4,8},{8,12},{12,16},{16,20},{20,24},{24,28},{1,5},{5,9},{9,... | collective-permute-start | bytes 393224 | tf_op jit(solution)/shard_map/ppermute | solution.py:16
  133.9 1.3 collective-permute-start.5
  135.2 0.1 fusion.41
  135.3 3.1 collective-permute-start.2
  138.4 2.7 collective-permute-start.3
  141.2 0.0 collective-permute-done.4
  141.2 8.3 %collective-permute-done.5 = f32[256,1,128]{0,2,1:T(8,128)S(1)} collective-permute-done((f32[256,1,128]{0,2,1:T(8,128)S(1)}, f32[256,1,128]{0,2,1:T(8,128)S(1)}, u32[]{:S(2)}, u32[]{:S(2)}) %collective-permute-start.5) | collective-permute-done | bytes 131104 | tf_op jit(solution)/shard_map/ppermute | solution.py:17
  149.5 3.1 collective-permute-start.6
  152.7 2.7 collective-permute-start.7
  155.4 0.0 collective-permute-done.2
  155.4 0.0 collective-permute-done.3
  155.4 0.0 copy-done.2
  155.4 1.5 fusion
  157.0 0.0 collective-permute-done.6
  157.0 1.3 collective-permute-done.7
  158.2 0.0 copy-done.3
  158.2 0.0 copy-done.4
  158.2 1.3 fusion.4
  159.6 2.0 convert_bitcast_fusion.1
  161.6 3.9 copy.20
  165.5 0.0 reduce-scatter.7.cloned.1.call-update
  165.6 0.0 all-gather.5.cloned.1.call-start
  165.6 105.7 %reduce-scatter.7.cloned.1.call-done = bf16[64,1024]{1,0:T(8,128)(2,1)} async-done(((bf16[1024,1024]{1,0:T(8,128)(2,1)}), bf16[64,1024]{1,0:T(8,128)(2,1)}) %reduce-scatter.7.cloned.1.call-update) | async-done | bytes 131088
  271.3 1.1 copy.21
  272.4 0.2 copy.17
  272.6 0.0 copy-done.1
  272.6 0.7 copy.31
  273.3 0.0 all-gather.5.cloned.1.call-update
  273.4 0.0 reduce-scatter.9.cloned.1.call-start
  273.4 94.9 %all-gather.5.cloned.1.call-done = bf16[1024,1024]{1,0:T(8,128)(2,1)} async-done(((bf16[64,1024]{1,0:T(8,128)(2,1)}), bf16[1024,1024]{1,0:T(8,128)(2,1)}) %all-gather.5.cloned.1.call-update) | async-done | bytes 2097168 | tf_op jit(solution)/shard_map/all_gather | solution.py:53
  368.3 2.4 fusion.44
  370.7 17.0 %collective-permute-start.8 = (f32[256,1,128]{0,2,1:T(8,128)S(1)}, f32[256,1,128]{0,2,1:T(8,128)S(1)}, u32[]{:S(2)}, u32[]{:S(2)}) collective-permute-start(f32[256,1,128]{0,2,1:T(8,128)S(1)} %get-tuple-element.9), channel_id=1, source_target_pairs={{0,4},{4,8},{8,12},{12,16},{16,20},{20,24},{24,28},{1,5},{5,9},{9,... | collective-permute-start | bytes 393224 | tf_op jit(solution)/shard_map/ppermute | solution.py:16
  387.7 1.3 collective-permute-start.9
  389.0 1.2 collective-permute-done.8
  390.1 13.1 %collective-permute-done.9 = f32[256,1,128]{0,2,1:T(8,128)S(1)} collective-permute-done((f32[256,1,128]{0,2,1:T(8,128)S(1)}, f32[256,1,128]{0,2,1:T(8,128)S(1)}, u32[]{:S(2)}, u32[]{:S(2)}) %collective-permute-start.9) | collective-permute-done | bytes 131104 | tf_op jit(solution)/shard_map/ppermute | solution.py:17
  403.2 1.9 collective-permute-start.10
  405.2 3.9 collective-permute-start.11
  409.1 0.0 collective-permute-done.10
  409.1 1.6 collective-permute-done.11
  410.7 1.3 fusion.8
  412.1 0.7 convert_bitcast_fusion
  412.8 2.6 copy.22
  415.4 0.0 reduce-scatter.9.cloned.1.call-update
  415.4 104.8 %reduce-scatter.9.cloned.1.call-done = bf16[64,1024]{1,0:T(8,128)(2,1)} async-done(((bf16[1024,1024]{1,0:T(8,128)(2,1)}), bf16[64,1024]{1,0:T(8,128)(2,1)}) %reduce-scatter.9.cloned.1.call-update) | async-done | bytes 131088
  520.2 1.1 copy.23
  521.4 0.2 copy.18
  521.6 0.7 convert_add_fusion
  (12 shorter events, 0.2 us)
Async XLA Ops:
  6.5 107.9 %copy-start = (bf16[256,1024]{1,0:T(8,128)(2,1)S(1)}, bf16[256,1024]{1,0:T(8,128)(2,1)}, u32[]{:S(2)}) copy-start(bf16[256,1024]{1,0:T(8,128)(2,1)} %param.7) | copy-start | bytes 1572868
  6.5 107.9 %all-gather.3.cloned.1.call-start = ((), (), s32[]{:S(2)}) async-start(), calls=%async_computation.2 | async-start | bytes 2228224 | tf_op jit(solution)/shard_map/all_gather | solution.py:53
  8.2 263.1 %reduce-scatter.7.cloned.1.call-start = ((), (), s32[]{:S(2)}) async-start(), calls=%async_computation.4 | async-start | bytes 2228224
  9.1 17.0 %collective-permute-start = (f32[8,1,128]{2,0,1:T(8,128)S(1)}, f32[8,1,128]{2,0,1:T(8,128)S(1)}, u32[]{:S(2)}, u32[]{:S(2)}) collective-permute-start(f32[8,1,128]{2,0,1:T(8,128)S(1)} %copy.29), channel_id=1, source_target_pairs={{0,4},{4,8},{8,12},{12,16},{16,20},{20,24},{24,28},{1,5},{5,9},{9,... | collective-permute-start | bytes 12296 | tf_op jit(solution)/shard_map/ppermute | solution.py:16
  24.8 14.3 %collective-permute-start.1 = (f32[8,1,128]{2,0,1:T(8,128)S(1)}, f32[8,1,128]{2,0,1:T(8,128)S(1)}, u32[]{:S(2)}, u32[]{:S(2)}) collective-permute-start(f32[8,1,128]{2,0,1:T(8,128)S(1)} %copy.30), channel_id=1, source_target_pairs={{4,0},{8,4},{12,8},{16,12},{20,16},{24,20},{28,24},{5,1},{9,5},{13... | collective-permute-start | bytes 12296 | tf_op jit(solution)/shard_map/ppermute | solution.py:17
  39.2 116.3 %copy-start.2 = (f32[256,8]{0,1:T(8,128)S(1)}, f32[256,8]{0,1:T(8,128)}, u32[]{:S(2)}) copy-start(f32[256,8]{0,1:T(8,128)} %param.9) | copy-start | bytes 24580
  117.0 41.2 %copy-start.3 = (f32[256]{0:T(256)S(1)}, f32[256]{0:T(256)}, u32[]{:S(2)}) copy-start(f32[256]{0:T(256)} %param.11) | copy-start | bytes 3076
  117.0 41.2 %copy-start.4 = (f32[256]{0:T(256)S(1)}, f32[256]{0:T(256)}, u32[]{:S(2)}) copy-start(f32[256]{0:T(256)} %param.8) | copy-start | bytes 3076
  117.1 24.1 %collective-permute-start.4 = (f32[256,1,128]{0,2,1:T(8,128)S(1)}, f32[256,1,128]{0,2,1:T(8,128)S(1)}, u32[]{:S(2)}, u32[]{:S(2)}) collective-permute-start(f32[256,1,128]{0,2,1:T(8,128)S(1)} %get-tuple-element.11), channel_id=1, source_target_pairs={{0,4},{4,8},{8,12},{12,16},{16,20},{20,24},{24,28},{1,5},{5,9},{9,... | collective-permute-start | bytes 393224 | tf_op jit(solution)/shard_map/ppermute | solution.py:16
  133.9 15.6 %collective-permute-start.5 = (f32[256,1,128]{0,2,1:T(8,128)S(1)}, f32[256,1,128]{0,2,1:T(8,128)S(1)}, u32[]{:S(2)}, u32[]{:S(2)}) collective-permute-start(f32[256,1,128]{0,2,1:T(8,128)S(1)} %get-tuple-element.12), channel_id=1, source_target_pairs={{4,0},{8,4},{12,8},{16,12},{20,16},{24,20},{28,24},{5,1},{9,5},{13... | collective-permute-start | bytes 393224 | tf_op jit(solution)/shard_map/ppermute | solution.py:17
  135.3 20.1 %collective-permute-start.2 = (f32[8,10,1]{2,0,1:T(8,128)S(1)}, f32[8,10,1]{2,0,1:T(8,128)S(1)}, u32[]{:S(2)}, u32[]{:S(2)}) collective-permute-start(f32[8,10,1]{2,0,1:T(8,128)S(1)} %get-tuple-element.13), channel_id=1, source_target_pairs={{0,1},{1,2},{2,3},{4,5},{5,6},{6,7},{8,9},{9,10},{10,11},{12,13},{... | collective-permute-start | bytes 968 | tf_op jit(solution)/shard_map/ppermute | solution.py:16
  138.4 17.0 %collective-permute-start.3 = (f32[8,10,1]{2,0,1:T(8,128)S(1)}, f32[8,10,1]{2,0,1:T(8,128)S(1)}, u32[]{:S(2)}, u32[]{:S(2)}) collective-permute-start(f32[8,10,1]{2,0,1:T(8,128)S(1)} %get-tuple-element.14), channel_id=1, source_target_pairs={{1,0},{2,1},{3,2},{5,4},{6,5},{7,6},{9,8},{10,9},{11,10},{13,12},{... | collective-permute-start | bytes 968 | tf_op jit(solution)/shard_map/ppermute | solution.py:17
  149.5 7.4 %collective-permute-start.6 = (f32[256,10,1]{0,2,1:T(1,128)S(1)}, f32[256,10,1]{0,2,1:T(1,128)S(1)}, u32[]{:S(2)}, u32[]{:S(2)}) collective-permute-start(f32[256,10,1]{0,2,1:T(1,128)S(1)} %get-tuple-element.7), channel_id=1, source_target_pairs={{0,1},{1,2},{2,3},{4,5},{5,6},{6,7},{8,9},{9,10},{10,11},{12,13},{... | collective-permute-start | bytes 30728 | tf_op jit(solution)/shard_map/ppermute | solution.py:16
  152.7 5.6 %collective-permute-start.7 = (f32[256,10,1]{0,2,1:T(1,128)S(1)}, f32[256,10,1]{0,2,1:T(1,128)S(1)}, u32[]{:S(2)}, u32[]{:S(2)}) collective-permute-start(f32[256,10,1]{0,2,1:T(1,128)S(1)} %get-tuple-element.8), channel_id=1, source_target_pairs={{1,0},{2,1},{3,2},{5,4},{6,5},{7,6},{9,8},{10,9},{11,10},{13,12},{... | collective-permute-start | bytes 30728 | tf_op jit(solution)/shard_map/ppermute | solution.py:17
  165.5 107.1 %copy-start.1 = (bf16[64,8,128]{2,1,0:T(8,128)(2,1)S(1)}, bf16[64,8,128]{2,1,0:T(8,128)(2,1)}, u32[]{:S(2)}) copy-start(bf16[64,8,128]{2,1,0:T(8,128)(2,1)} %param.6) | copy-start | bytes 393220
  165.6 202.7 %all-gather.5.cloned.1.call-start = ((), (), s32[]{:S(2)}) async-start(), calls=%async_computation.3 | async-start | bytes 2228224 | tf_op jit(solution)/shard_map/all_gather | solution.py:53
  273.4 246.9 %reduce-scatter.9.cloned.1.call-start = ((), (), s32[]{:S(2)}) async-start(), calls=%async_computation.5 | async-start | bytes 2228224
  370.7 19.5 %collective-permute-start.8 = (f32[256,1,128]{0,2,1:T(8,128)S(1)}, f32[256,1,128]{0,2,1:T(8,128)S(1)}, u32[]{:S(2)}, u32[]{:S(2)}) collective-permute-start(f32[256,1,128]{0,2,1:T(8,128)S(1)} %get-tuple-element.9), channel_id=1, source_target_pairs={{0,4},{4,8},{8,12},{12,16},{16,20},{20,24},{24,28},{1,5},{5,9},{9,... | collective-permute-start | bytes 393224 | tf_op jit(solution)/shard_map/ppermute | solution.py:16
  387.7 15.6 %collective-permute-start.9 = (f32[256,1,128]{0,2,1:T(8,128)S(1)}, f32[256,1,128]{0,2,1:T(8,128)S(1)}, u32[]{:S(2)}, u32[]{:S(2)}) collective-permute-start(f32[256,1,128]{0,2,1:T(8,128)S(1)} %get-tuple-element.10), channel_id=1, source_target_pairs={{4,0},{8,4},{12,8},{16,12},{20,16},{24,20},{28,24},{5,1},{9,5},{13... | collective-permute-start | bytes 393224 | tf_op jit(solution)/shard_map/ppermute | solution.py:17
  403.2 5.9 %collective-permute-start.10 = (f32[256,10,1]{0,2,1:T(1,128)S(1)}, f32[256,10,1]{0,2,1:T(1,128)S(1)}, u32[]{:S(2)}, u32[]{:S(2)}) collective-permute-start(f32[256,10,1]{0,2,1:T(1,128)S(1)} %get-tuple-element.5), channel_id=1, source_target_pairs={{0,1},{1,2},{2,3},{4,5},{5,6},{6,7},{8,9},{9,10},{10,11},{12,13},{... | collective-permute-start | bytes 30728 | tf_op jit(solution)/shard_map/ppermute | solution.py:16
  405.2 5.6 %collective-permute-start.11 = (f32[256,10,1]{0,2,1:T(1,128)S(1)}, f32[256,10,1]{0,2,1:T(1,128)S(1)}, u32[]{:S(2)}, u32[]{:S(2)}) collective-permute-start(f32[256,10,1]{0,2,1:T(1,128)S(1)} %get-tuple-element.6), channel_id=1, source_target_pairs={{1,0},{2,1},{3,2},{5,4},{6,5},{7,6},{9,8},{10,9},{11,10},{13,12},{... | collective-permute-start | bytes 30728 | tf_op jit(solution)/shard_map/ppermute | solution.py:17
Sparse Core Ops, SparseCore 0:
  9.4 105.0 all-gather.2
  165.7 105.5 reduce-scatter.6
  273.5 94.7 all-gather.4
  415.5 104.6 reduce-scatter.8
where the time goes:
time: 530 us; the launch traced here: 529 us
  waiting for transfers between devices  418 us (79%)
  starting transfers between devices  71.1 us (13%)
  between operations  13.4 us (3%)
  local copies, waits for them, and re-layouts  13.1 us (2%)
  matrix products  9.15 us (2%)
    unnamed x6, waiting for transfers between devices  211 us
    all_gather x2, waiting for transfers between devices, realize(): lax.all_gather(block_flat, 'quad', axis=0, tiled=True)  170 us
    ppermute x6, starting transfers between devices, with_halo(): before = lax.ppermute(last, axis, up)  57.7 us
    ppermute x6, waiting for transfers between devices, with_halo(): after = lax.ppermute(leading, axis, down)  36.5 us
    ppermute x6, starting transfers between devices, with_halo(): after = lax.ppermute(leading, axis, down)  13.2 us
    unnamed x20, local copies, waits for them, and re-layouts  11.8 us
  transfers between devices with their start and end apart: 16, of which 10 were waited for; matrix products, arithmetic and copies ran while one was open for 1% of the time, Pallas kernels for 0%

commit v1 on v0

--- a/solution.py
+++ b/solution.py
@@ -4,6 +4,13 @@
 from jax.sharding import PartitionSpec as P
 
 time_step = 0.04
+
+
+def swapped_in(x, axis, dim):
+    peers = lax.axis_size(axis)
+    shards = jnp.stack([x for _ in range(peers)])
+    shards = lax.all_to_all(shards, axis, split_axis=0, concat_axis=0)
+    return jnp.concatenate(shards, axis=dim)
 
 
 def with_halo(array, sides, width):
@@ -49,9 +56,7 @@
 
     def realize(block_flat):
         return jnp.dot(
-            basis_rows,
-            lax.all_gather(block_flat, "quad", axis=0, tiled=True),
-            preferred_element_type=jnp.float32,
+            basis_rows, swapped_in(block_flat, "quad", 0), preferred_element_type=jnp.float32
         )
 
     def field_of(block):

time: 530 us -> 547 us (1.032)
  the two profiles are of different devices: /device:TPU:4 before, /device:TPU:2 now
where the time goes in v1:
time: 547 us; the launch traced here: 546 us
  waiting for transfers between devices  348 us (64%)
  blocking collectives  96.9 us (18%)
  starting transfers between devices  62.4 us (11%)
  local copies, waits for them, and re-layouts  16.2 us (3%)
  between operations  13.8 us (3%)
  matrix products  5.78 us (1%)
    unnamed x4, waiting for transfers between devices  247 us
    all_to_all x1, blocking collectives, swapped_in(): shards = lax.all_to_all(shards, axis, split_axis=0, concat_axis=0)  96.9 us
    ppermute x6, starting transfers between devices, with_halo(): before = lax.ppermute(last, axis, up)  38.3 us
    ppermute x6, waiting for transfers between devices, with_halo(): before = lax.ppermute(last, axis, up)  36 us
    all_to_all x1, waiting for transfers between devices, swapped_in(): shards = lax.all_to_all(shards, axis, split_axis=0, concat_axis=0)  33 us
    ppermute x6, waiting for transfers between devices, with_halo(): after = lax.ppermute(leading, axis, down)  32.4 us
    all_to_all x1, starting transfers between devices, swapped_in(): shards = lax.all_to_all(shards, axis, split_axis=0, concat_axis=0)  12.8 us
    ppermute x6, starting transfers between devices, with_halo(): after = lax.ppermute(leading, axis, down)  11.3 us
  transfers between devices with their start and end apart: 15, of which 10 were waited for; matrix products, arithmetic and copies ran while one was open for 0% of the time, Pallas kernels for 0%

profile of v1, /device:TPU:2, one launch (start us, length us, event | category | flops | bytes accessed | tf_op | source)
XLA Modules:
  0.0 546.5 jit_solution(3365145714008128622)
XLA Ops:
  6.5 0.0 copy-start
  6.5 1.0 copy.37
  7.5 1.6 stack.6
  9.1 0.0 copy-start.3
  9.1 12.8 %all-to-all-start = ((bf16[16,64,1024]{2,1,0:T(8,128)(2,1)}), bf16[16,64,1024]{2,1,0:T(8,128)(2,1)S(1)}, u32[]{:S(2)}, u32[]{:S(2)}) async-start(bf16[16,64,1024]{2,1,0:T(8,128)(2,1)} %stack.6), calls=%async_computation | async-start | bytes 4194304 | tf_op jit(solution)/shard_map/all_to_all | solution.py:12
  21.9 0.0 reduce-scatter.7.cloned.1.call-start
  21.9 0.0 copy-done.3
  22.0 8.2 %collective-permute-start = (f32[8,1,128]{2,0,1:T(8,128)S(1)}, f32[8,1,128]{2,0,1:T(8,128)S(1)}, u32[]{:S(2)}, u32[]{:S(2)}) collective-permute-start(f32[8,1,128]{2,0,1:T(8,128)S(1)} %copy.34), channel_id=1, source_target_pairs={{0,4},{4,8},{8,12},{12,16},{16,20},{20,24},{24,28},{1,5},{5,9},{9,... | collective-permute-start | bytes 12296 | tf_op jit(solution)/shard_map/ppermute | solution.py:23
  30.2 1.3 collective-permute-start.1
  31.5 31.3 %collective-permute-done = f32[8,1,128]{2,0,1:T(8,128)S(1)} collective-permute-done((f32[8,1,128]{2,0,1:T(8,128)S(1)}, f32[8,1,128]{2,0,1:T(8,128)S(1)}, u32[]{:S(2)}, u32[]{:S(2)}) %collective-permute-start) | collective-permute-done | bytes 4128 | tf_op jit(solution)/shard_map/ppermute | solution.py:23
  62.8 7.1 %collective-permute-done.1 = f32[8,1,128]{2,0,1:T(8,128)S(1)} collective-permute-done((f32[8,1,128]{2,0,1:T(8,128)S(1)}, f32[8,1,128]{2,0,1:T(8,128)S(1)}, u32[]{:S(2)}, u32[]{:S(2)}) %collective-permute-start.1) | collective-permute-done | bytes 4128 | tf_op jit(solution)/shard_map/ppermute | solution.py:24
  69.9 33.0 %all-to-all-done = bf16[16,64,1024]{2,1,0:T(8,128)(2,1)S(1)} async-done(((bf16[16,64,1024]{2,1,0:T(8,128)(2,1)}), bf16[16,64,1024]{2,1,0:T(8,128)(2,1)S(1)}, u32[]{:S(2)}, u32[]{:S(2)}) %all-to-all-start) | async-done | bytes 2097184 | tf_op jit(solution)/shard_map/all_to_all | solution.py:12
  102.8 1.3 copy-done.1
  104.1 2.9 copy.22
  107.0 0.0 copy-done
  107.0 0.0 copy-start.4
  107.0 0.7 fusion.31
  107.8 0.0 copy-start.5
  107.8 0.0 copy-start.6
  107.8 8.2 %collective-permute-start.4 = (f32[256,1,128]{0,2,1:T(8,128)S(1)}, f32[256,1,128]{0,2,1:T(8,128)S(1)}, u32[]{:S(2)}, u32[]{:S(2)}) collective-permute-start(f32[256,1,128]{0,2,1:T(8,128)S(1)} %get-tuple-element.11), channel_id=1, source_target_pairs={{0,4},{4,8},{8,12},{12,16},{16,20},{20,24},{24,28},{1,5},{5,9},{9,... | collective-permute-start | bytes 393224 | tf_op jit(solution)/shard_map/ppermute | solution.py:23
  116.1 1.3 collective-permute-start.5
  117.4 0.1 fusion.43
  117.5 3.4 collective-permute-start.2
  120.9 2.4 collective-permute-start.3
  123.3 0.0 collective-permute-done.4
  123.3 9.6 %collective-permute-done.5 = f32[256,1,128]{0,2,1:T(8,128)S(1)} collective-permute-done((f32[256,1,128]{0,2,1:T(8,128)S(1)}, f32[256,1,128]{0,2,1:T(8,128)S(1)}, u32[]{:S(2)}, u32[]{:S(2)}) %collective-permute-start.5) | collective-permute-done | bytes 131104 | tf_op jit(solution)/shard_map/ppermute | solution.py:24
  132.9 3.4 collective-permute-start.6
  136.3 2.4 collective-permute-start.7
  138.7 0.0 collective-permute-done.2
  138.8 0.0 collective-permute-done.3
  138.8 0.0 copy-done.4
  138.8 1.5 fusion
  140.3 0.0 collective-permute-done.6
  140.3 1.5 collective-permute-done.7
  141.9 0.0 copy-done.5
  141.9 0.0 copy-done.6
  141.9 1.3 fusion.4
  143.2 2.0 convert_bitcast_fusion.1
  145.2 3.9 copy.25
  149.2 0.0 reduce-scatter.7.cloned.1.call-update
  149.2 0.0 reduce-scatter.9.cloned.1.call-start
  149.2 128.5 %reduce-scatter.7.cloned.1.call-done = bf16[64,1024]{1,0:T(8,128)(2,1)} async-done(((bf16[1024,1024]{1,0:T(8,128)(2,1)}), bf16[64,1024]{1,0:T(8,128)(2,1)}) %reduce-scatter.7.cloned.1.call-update) | async-done | bytes 131088
  277.7 1.1 copy.26
  278.8 0.2 copy.23
  279.0 0.0 copy-done.2
  279.1 0.3 stack.7
  279.4 96.9 %all_to_all.10 = bf16[16,64,1024]{2,1,0:T(8,128)(2,1)S(1)} all-to-all(bf16[16,64,1024]{2,1,0:T(8,128)(2,1)S(1)} %stack.7), channel_id=1, replica_groups=mesh['quad'=16,'gy'=8,'gx'=4] {'quad'}, dimensions={0} | all-to-all | bytes 4194304 | tf_op jit(solution)/shard_map/all_to_all | solution.py:12
  376.2 0.8 fusion.45
  377.0 11.8 %collective-permute-start.8 = (f32[256,1,128]{0,2,1:T(8,128)S(1)}, f32[256,1,128]{0,2,1:T(8,128)S(1)}, u32[]{:S(2)}, u32[]{:S(2)}) collective-permute-start(f32[256,1,128]{0,2,1:T(8,128)S(1)} %get-tuple-element.9), channel_id=1, source_target_pairs={{0,4},{4,8},{8,12},{12,16},{16,20},{20,24},{24,28},{1,5},{5,9},{9,... | collective-permute-start | bytes 393224 | tf_op jit(solution)/shard_map/ppermute | solution.py:23
  388.8 1.3 collective-permute-start.9
  390.1 4.8 collective-permute-done.8
  394.8 11.2 %collective-permute-done.9 = f32[256,1,128]{0,2,1:T(8,128)S(1)} collective-permute-done((f32[256,1,128]{0,2,1:T(8,128)S(1)}, f32[256,1,128]{0,2,1:T(8,128)S(1)}, u32[]{:S(2)}, u32[]{:S(2)}) %collective-permute-start.9) | collective-permute-done | bytes 131104 | tf_op jit(solution)/shard_map/ppermute | solution.py:24
  406.1 3.3 collective-permute-start.10
  409.4 2.5 collective-permute-start.11
  411.9 0.0 collective-permute-done.10
  411.9 3.0 collective-permute-done.11
  414.9 1.3 fusion.8
  416.3 0.7 convert_bitcast_fusion
  417.0 2.6 copy.27
  419.6 0.0 reduce-scatter.9.cloned.1.call-update
  419.6 118.0 %reduce-scatter.9.cloned.1.call-done = bf16[64,1024]{1,0:T(8,128)(2,1)} async-done(((bf16[1024,1024]{1,0:T(8,128)(2,1)}), bf16[64,1024]{1,0:T(8,128)(2,1)}) %reduce-scatter.9.cloned.1.call-update) | async-done | bytes 131088
  537.6 1.1 copy.28
  538.7 0.2 copy.24
  538.9 0.7 convert_add_fusion
  (16 shorter events, 0.2 us)
Async XLA Ops:
  6.5 100.5 %copy-start = (bf16[256,1024]{1,0:T(8,128)(2,1)S(1)}, bf16[256,1024]{1,0:T(8,128)(2,1)}, u32[]{:S(2)}) copy-start(bf16[256,1024]{1,0:T(8,128)(2,1)} %param.7) | copy-start | bytes 1572868
  9.1 12.8 %copy-start.3 = (f32[8,8,128]{2,1,0:T(8,128)S(1)}, f32[8,8,128]{2,1,0:T(8,128)}, u32[]{:S(2)}) copy-start(f32[8,8,128]{2,1,0:T(8,128)} %param.10) | copy-start | bytes 98308
  9.1 93.7 %all-to-all-start = ((bf16[16,64,1024]{2,1,0:T(8,128)(2,1)}), bf16[16,64,1024]{2,1,0:T(8,128)(2,1)S(1)}, u32[]{:S(2)}, u32[]{:S(2)}) async-start(bf16[16,64,1024]{2,1,0:T(8,128)(2,1)} %stack.6), calls=%async_computation | async-start | bytes 4194304 | tf_op jit(solution)/shard_map/all_to_all | solution.py:12
  21.9 255.8 %reduce-scatter.7.cloned.1.call-start = ((), (), s32[]{:S(2)}) async-start(), calls=%async_computation.4 | async-start | bytes 2228224
  22.0 40.8 %collective-permute-start = (f32[8,1,128]{2,0,1:T(8,128)S(1)}, f32[8,1,128]{2,0,1:T(8,128)S(1)}, u32[]{:S(2)}, u32[]{:S(2)}) collective-permute-start(f32[8,1,128]{2,0,1:T(8,128)S(1)} %copy.34), channel_id=1, source_target_pairs={{0,4},{4,8},{8,12},{12,16},{16,20},{20,24},{24,28},{1,5},{5,9},{9,... | collective-permute-start | bytes 12296 | tf_op jit(solution)/shard_map/ppermute | solution.py:23
  30.2 39.7 %collective-permute-start.1 = (f32[8,1,128]{2,0,1:T(8,128)S(1)}, f32[8,1,128]{2,0,1:T(8,128)S(1)}, u32[]{:S(2)}, u32[]{:S(2)}) collective-permute-start(f32[8,1,128]{2,0,1:T(8,128)S(1)} %copy.35), channel_id=1, source_target_pairs={{4,0},{8,4},{12,8},{16,12},{20,16},{24,20},{28,24},{5,1},{9,5},{13... | collective-permute-start | bytes 12296 | tf_op jit(solution)/shard_map/ppermute | solution.py:24
  102.8 1.3 copy-start.1
  107.0 31.8 %copy-start.4 = (f32[256,8]{0,1:T(8,128)S(1)}, f32[256,8]{0,1:T(8,128)}, u32[]{:S(2)}) copy-start(f32[256,8]{0,1:T(8,128)} %param.9) | copy-start | bytes 24580
  107.8 34.1 %copy-start.5 = (f32[256]{0:T(256)S(1)}, f32[256]{0:T(256)}, u32[]{:S(2)}) copy-start(f32[256]{0:T(256)} %param.11) | copy-start | bytes 3076
  107.8 34.1 %copy-start.6 = (f32[256]{0:T(256)S(1)}, f32[256]{0:T(256)}, u32[]{:S(2)}) copy-start(f32[256]{0:T(256)} %param.8) | copy-start | bytes 3076
  107.8 15.5 %collective-permute-start.4 = (f32[256,1,128]{0,2,1:T(8,128)S(1)}, f32[256,1,128]{0,2,1:T(8,128)S(1)}, u32[]{:S(2)}, u32[]{:S(2)}) collective-permute-start(f32[256,1,128]{0,2,1:T(8,128)S(1)} %get-tuple-element.11), channel_id=1, source_target_pairs={{0,4},{4,8},{8,12},{12,16},{16,20},{20,24},{24,28},{1,5},{5,9},{9,... | collective-permute-start | bytes 393224 | tf_op jit(solution)/shard_map/ppermute | solution.py:23
  116.1 16.8 %collective-permute-start.5 = (f32[256,1,128]{0,2,1:T(8,128)S(1)}, f32[256,1,128]{0,2,1:T(8,128)S(1)}, u32[]{:S(2)}, u32[]{:S(2)}) collective-permute-start(f32[256,1,128]{0,2,1:T(8,128)S(1)} %get-tuple-element.12), channel_id=1, source_target_pairs={{4,0},{8,4},{12,8},{16,12},{20,16},{24,20},{28,24},{5,1},{9,5},{13... | collective-permute-start | bytes 393224 | tf_op jit(solution)/shard_map/ppermute | solution.py:24
  117.5 21.3 %collective-permute-start.2 = (f32[8,10,1]{2,0,1:T(8,128)S(1)}, f32[8,10,1]{2,0,1:T(8,128)S(1)}, u32[]{:S(2)}, u32[]{:S(2)}) collective-permute-start(f32[8,10,1]{2,0,1:T(8,128)S(1)} %get-tuple-element.13), channel_id=1, source_target_pairs={{0,1},{1,2},{2,3},{4,5},{5,6},{6,7},{8,9},{9,10},{10,11},{12,13},{... | collective-permute-start | bytes 968 | tf_op jit(solution)/shard_map/ppermute | solution.py:23
  120.9 17.9 %collective-permute-start.3 = (f32[8,10,1]{2,0,1:T(8,128)S(1)}, f32[8,10,1]{2,0,1:T(8,128)S(1)}, u32[]{:S(2)}, u32[]{:S(2)}) collective-permute-start(f32[8,10,1]{2,0,1:T(8,128)S(1)} %get-tuple-element.14), channel_id=1, source_target_pairs={{1,0},{2,1},{3,2},{5,4},{6,5},{7,6},{9,8},{10,9},{11,10},{13,12},{... | collective-permute-start | bytes 968 | tf_op jit(solution)/shard_map/ppermute | solution.py:24
  132.9 7.4 %collective-permute-start.6 = (f32[256,10,1]{0,2,1:T(1,128)S(1)}, f32[256,10,1]{0,2,1:T(1,128)S(1)}, u32[]{:S(2)}, u32[]{:S(2)}) collective-permute-start(f32[256,10,1]{0,2,1:T(1,128)S(1)} %get-tuple-element.7), channel_id=1, source_target_pairs={{0,1},{1,2},{2,3},{4,5},{5,6},{6,7},{8,9},{9,10},{10,11},{12,13},{... | collective-permute-start | bytes 30728 | tf_op jit(solution)/shard_map/ppermute | solution.py:23
  136.3 5.6 %collective-permute-start.7 = (f32[256,10,1]{0,2,1:T(1,128)S(1)}, f32[256,10,1]{0,2,1:T(1,128)S(1)}, u32[]{:S(2)}, u32[]{:S(2)}) collective-permute-start(f32[256,10,1]{0,2,1:T(1,128)S(1)} %get-tuple-element.8), channel_id=1, source_target_pairs={{1,0},{2,1},{3,2},{5,4},{6,5},{7,6},{9,8},{10,9},{11,10},{13,12},{... | collective-permute-start | bytes 30728 | tf_op jit(solution)/shard_map/ppermute | solution.py:24
  149.1 129.9 %copy-start.2 = (bf16[64,8,128]{2,1,0:T(8,128)(2,1)S(1)}, bf16[64,8,128]{2,1,0:T(8,128)(2,1)}, u32[]{:S(2)}) copy-start(bf16[64,8,128]{2,1,0:T(8,128)(2,1)} %param.6) | copy-start | bytes 393220
  149.2 388.4 %reduce-scatter.9.cloned.1.call-start = ((), (), s32[]{:S(2)}) async-start(), calls=%async_computation.5 | async-start | bytes 2228224
  377.0 17.8 %collective-permute-start.8 = (f32[256,1,128]{0,2,1:T(8,128)S(1)}, f32[256,1,128]{0,2,1:T(8,128)S(1)}, u32[]{:S(2)}, u32[]{:S(2)}) collective-permute-start(f32[256,1,128]{0,2,1:T(8,128)S(1)} %get-tuple-element.9), channel_id=1, source_target_pairs={{0,4},{4,8},{8,12},{12,16},{16,20},{20,24},{24,28},{1,5},{5,9},{9,... | collective-permute-start | bytes 393224 | tf_op jit(solution)/shard_map/ppermute | solution.py:23
  388.8 17.2 %collective-permute-start.9 = (f32[256,1,128]{0,2,1:T(8,128)S(1)}, f32[256,1,128]{0,2,1:T(8,128)S(1)}, u32[]{:S(2)}, u32[]{:S(2)}) collective-permute-start(f32[256,1,128]{0,2,1:T(8,128)S(1)} %get-tuple-element.10), channel_id=1, source_target_pairs={{4,0},{8,4},{12,8},{16,12},{20,16},{24,20},{28,24},{5,1},{9,5},{13... | collective-permute-start | bytes 393224 | tf_op jit(solution)/shard_map/ppermute | solution.py:24
  406.1 5.9 %collective-permute-start.10 = (f32[256,10,1]{0,2,1:T(1,128)S(1)}, f32[256,10,1]{0,2,1:T(1,128)S(1)}, u32[]{:S(2)}, u32[]{:S(2)}) collective-permute-start(f32[256,10,1]{0,2,1:T(1,128)S(1)} %get-tuple-element.5), channel_id=1, source_target_pairs={{0,1},{1,2},{2,3},{4,5},{5,6},{6,7},{8,9},{9,10},{10,11},{12,13},{... | collective-permute-start | bytes 30728 | tf_op jit(solution)/shard_map/ppermute | solution.py:23
  409.4 5.6 %collective-permute-start.11 = (f32[256,10,1]{0,2,1:T(1,128)S(1)}, f32[256,10,1]{0,2,1:T(1,128)S(1)}, u32[]{:S(2)}, u32[]{:S(2)}) collective-permute-start(f32[256,10,1]{0,2,1:T(1,128)S(1)} %get-tuple-element.6), channel_id=1, source_target_pairs={{1,0},{2,1},{3,2},{5,4},{6,5},{7,6},{9,8},{10,9},{11,10},{13,12},{... | collective-permute-start | bytes 30728 | tf_op jit(solution)/shard_map/ppermute | solution.py:24
Sparse Core Ops, SparseCore 0:
  149.3 128.3 reduce-scatter.6
  419.7 117.8 reduce-scatter.8
